TPU v7x, 32 devices: a whole 2x2x4 slice. The times are simulated.
32 devices in a mesh: vocab: 8 (over y, x, core), width: 4 (over z).
Axes of the slice: x: 2, y: 2, z: 4, core: 2. Of those that a mesh axis runs over, the one named last changes fastest.
Arguments:
- hidden: bfloat16 [256, 2880], P('width'), may hold values from -60 to 60
- gain: float32 [2880], replicated, may hold values from 0.1 to 1.9
- unembed: bfloat16 [2880, 50176], P('width', 'vocab'), may hold values from -8 to 8
- targets: int32 [256], replicated, may hold values from 0 to 50175
- seq_ids: int32 [256], replicated, may hold values from 0 to 47, as said below
Outputs:
- log_normalizer: float32 [256], P('width')
- entropy: float32 [256], P('width')
- token_logprob: float32 [256], P('width')
- seq_mean: float32 [48], replicated
Inputs may be any that keep to these rules, and one draw needn't show every extreme that they name: `seq_ids`: rows of one sequence are consecutive and ids never fall; every sequence has at least one row.
All inputs are finite; a program needn't handle non-finite values.
Results may differ from a plain program's by a relative error of at most 0.0014.
Values may be sent and summed in bfloat16 or wider, within the bound.
A program may use at most 128 MiB of HBM per device.

v0:
```python
import jax
import jax.numpy as jnp
from jax import lax
from jax.sharding import PartitionSpec as P

SEQS = 48


def merged(part, axis, combine):
    gathered = jax.tree.map(lambda a: lax.all_gather(a, axis), part)

    def take(source):
        return jax.tree.map(lambda a: lax.dynamic_index_in_dim(a, source, 0, False), gathered)

    return lax.fori_loop(
        1, lax.axis_size(axis), lambda source, state: combine(state, take(source)), take(0)
    )


def combine_parts(first_part, second_part):
    merged_max = jnp.maximum(first_part[0], second_part[0])
    left_scale = jnp.exp(first_part[0] - merged_max)
    right_scale = jnp.exp(second_part[0] - merged_max)
    return (
        merged_max,
        first_part[1] * left_scale + second_part[1] * right_scale,
        first_part[2] * left_scale + second_part[2] * right_scale,
        first_part[3] + second_part[3],
    )


def local_stats(logits, wanted, first_col):
    column = first_col + lax.broadcasted_iota(jnp.int32, logits.shape, 1)
    target_hit = jnp.sum(jnp.where(column == wanted[:, None], logits, 0.0), axis=1)
    local_max = jnp.max(logits, axis=1)
    shifted = jnp.exp(logits - local_max[:, None])
    return (local_max, jnp.sum(shifted, axis=1), jnp.sum(shifted * logits, axis=1), target_hit)


def local(hidden, gain, unembed, targets, seq_ids):
    widths = lax.axis_size("width")
    owner = lax.axis_index("width")
    own_rows = hidden.shape[0]
    values = hidden.astype(jnp.float32)
    square = jnp.mean(values * values, axis=1, keepdims=True)
    normed = (values * lax.rsqrt(square + 1e-05) * gain[None, :]).astype(jnp.bfloat16)
    columns = lax.all_to_all(unembed, "width", split_axis=1, concat_axis=0, tiled=True)
    col_share = columns.shape[1]
    first_col = (lax.axis_index("vocab") * widths + owner) * col_share
    logits = jnp.dot(
        lax.all_gather(normed, "width", axis=0, tiled=True),
        columns,
        preferred_element_type=jnp.float32,
    )
    stats = local_stats(logits, targets, first_col)
    all_max, all_total, all_weighted, all_target = merged(stats, ("vocab", "width"), combine_parts)
    row_start = owner * own_rows
    row_max = lax.dynamic_slice_in_dim(all_max, row_start, own_rows, 0)
    exp_total = lax.dynamic_slice_in_dim(all_total, row_start, own_rows, 0)
    weighted = lax.dynamic_slice_in_dim(all_weighted, row_start, own_rows, 0)
    target_logit = lax.dynamic_slice_in_dim(all_target, row_start, own_rows, 0)
    log_normalizer = row_max + jnp.log(exp_total)
    entropy = log_normalizer - weighted / exp_total
    token_logprob = target_logit - log_normalizer
    own_seq = lax.dynamic_slice_in_dim(seq_ids, owner * own_rows, own_rows, 0)
    member = (own_seq[:, None] == jnp.arange(SEQS, dtype=jnp.int32)[None, :]).astype(jnp.float32)
    seq_sums, seq_counts = lax.psum(
        (jnp.dot(token_logprob, member, precision=lax.Precision.HIGHEST), jnp.sum(member, axis=0)),
        "width",
    )
    return (log_normalizer, entropy, token_logprob, seq_sums / seq_counts)


def solution(mesh):
    placed = (P("width", None), P(), P("width", "vocab"), P(), P())
    return jax.shard_map(
        local,
        mesh=mesh,
        in_specs=placed,
        out_specs=(P("width"), P("width"), P("width"), P()),
        check_vma=False,
    )
```

profile of v0, /device:TPU:0, one launch (start us, length us, event | category | flops | bytes accessed | tf_op | source)
XLA Modules:
  0.0 563.2 jit_solution(9940677662002967480)
XLA Ops:
  7.2 16.7 %all_to_all.14 = bf16[720,4,1568]{2,1,0:T(4,128)(2,1)} reshape(bf16[720,6272]{1,0:T(8,128)(2,1)} %param.9) | data formatting | bytes 18063360 | tf_op jit(solution)/shard_map/all_to_all | solution.py:47
  23.9 8.6 %copy.11 = bf16[720,4,1568]{2,0,1:T(8,128)(2,1)} copy(bf16[720,4,1568]{2,1,0:T(4,128)(2,1)} %all_to_all.14) | data formatting | bytes 18063360 | tf_op jit(solution)/shard_map/all_to_all | solution.py:47
  32.5 6.5 %all-to-all-start = ((bf16[720,4,1568]{2,0,1:T(8,128)(2,1)}), bf16[720,4,1568]{2,0,1:T(8,128)(2,1)}, u32[]{:S(2)}, u32[]{:S(2)}) async-start(bf16[720,4,1568]{2,0,1:T(8,128)(2,1)} %copy.11), calls=%async_computation | async-start | bytes 19169280 | tf_op jit(solution)/shard_map/all_to_all | solution.py:47
  39.0 0.0 all-gather.10.cloned.1.call-start
  39.0 0.0 copy-done
  39.0 0.2 fusion.1
  39.2 0.9 fusion.3
  40.1 0.0 all-gather.10.cloned.1.call-update
  40.1 0.1 dynamic_slice.76
  40.2 0.1 convert_reduce_fusion
  40.3 92.2 %all-gather.10.cloned.1.call-done = bf16[256,2880]{1,0:T(8,128)(2,1)} async-done(((bf16[64,2880]{1,0:T(8,128)(2,1)}), bf16[256,2880]{1,0:T(8,128)(2,1)}) %all-gather.10.cloned.1.call-update) | async-done | bytes 1474576 | tf_op jit(solution)/shard_map/all_gather | solution.py:51
  132.5 140.6 %all-to-all-done = bf16[720,4,1568]{2,0,1:T(8,128)(2,1)} async-done(((bf16[720,4,1568]{2,0,1:T(8,128)(2,1)}), bf16[720,4,1568]{2,0,1:T(8,128)(2,1)}, u32[]{:S(2)}, u32[]{:S(2)}) %all-to-all-start) | async-done | bytes 9031712 | tf_op jit(solution)/shard_map/all_to_all | solution.py:47
  273.1 8.2 %fusion.6 = (f32[256]{0:T(256)S(1)}, f32[256,1568]{0,1:T(8,128)S(1)}) fusion(bf16[256,2880]{1,0:T(8,128)(2,1)} %all-gather.10.cloned.1.call-done, bf16[2880,1568]{1,0:T(8,128)(2,1)} %bitcast.5), kind=kOutput, calls=%fused_computation.31 | convolution fusion | flops 2312511232 | bytes 12112896 | tf_op jit(solution)/shard_map/dot_general | solution.py:50
  281.4 0.9 multiply_reduce_fusion
  282.3 65.5 %all-gather.6 = f32[32,1,256]{2,1,0:T(1,128)S(1)} all-gather(f32[1,1,256]{2,1,0:T(1,128)S(1)} %bitcast.58), channel_id=4, replica_groups=mesh['vocab'=8,'width'=4] {'vocab','width'}, dimensions={0}, use_global_device_ids=true | all-gather | bytes 33792 | tf_op jit(solution)/shard_map/all_gather | solution.py:10
  347.8 63.9 %all-gather.7 = f32[32,1,256]{2,1,0:T(1,128)S(1)} all-gather(f32[1,1,256]{2,1,0:T(1,128)S(1)} %bitcast.57), channel_id=5, replica_groups=mesh['vocab'=8,'width'=4] {'vocab','width'}, dimensions={0}, use_global_device_ids=true | all-gather | bytes 33792 | tf_op jit(solution)/shard_map/all_gather | solution.py:10
  411.7 65.5 %all-gather.5 = f32[32,1,256]{2,1,0:T(1,128)S(1)} all-gather(f32[1,1,256]{2,1,0:T(1,128)S(1)} %bitcast.56), channel_id=3, replica_groups=mesh['vocab'=8,'width'=4] {'vocab','width'}, dimensions={0}, use_global_device_ids=true | all-gather | bytes 33792 | tf_op jit(solution)/shard_map/all_gather | solution.py:10
  477.1 63.9 %all-gather.4 = f32[32,1,256]{2,1,0:T(1,128)S(1)} all-gather(f32[1,1,256]{2,1,0:T(1,128)S(1)} %bitcast.55), channel_id=2, replica_groups=mesh['vocab'=8,'width'=4] {'vocab','width'}, dimensions={0}, use_global_device_ids=true | all-gather | bytes 33792 | tf_op jit(solution)/shard_map/all_gather | solution.py:10
  541.0 3.7 while.21
  544.7 0.1 dynamic-slice_subtract_fusion
  544.8 0.1 convolution_bitcast_fusion
  544.9 10.3 %all-reduce = (f32[48]{0:T(128)S(1)}, f32[48]{0:T(128)S(1)}) all-reduce(f32[48]{0:T(128)S(1)} %convolution_bitcast_fusion, f32[48]{0:T(128)S(1)} %convert_reduce_fusion), channel_id=1, replica_groups=mesh['vocab'=8,'width'=4] {'width'}, use_global_device_ids=true, to_apply=%region_7.8 | all-reduce | flops 96 | bytes 768 | tf_op jit(solution)/shard_map/psum | solution.py:67
  555.3 0.5 div.15
  555.8 0.6 divide_subtract_fusion
  (207 shorter events, 2.2 us)
Async XLA Ops:
  32.5 6.5 %copy-start = (bf16[64,2880]{1,0:T(8,128)(2,1)S(1)}, bf16[64,2880]{1,0:T(8,128)(2,1)}, u32[]{:S(2)}) copy-start(bf16[64,2880]{1,0:T(8,128)(2,1)} %param.7) | copy-start | bytes 1105924
  32.5 6.7 %copy-start.1 = (f32[2880]{0:T(1024)S(1)}, f32[2880]{0:T(1024)}, u32[]{:S(2)}) copy-start(f32[2880]{0:T(1024)} %param.8) | copy-start | bytes 34564
  32.5 7.6 %copy-start.5 = (s32[256]{0:T(256)S(1)}, s32[256]{0:T(256)}, u32[]{:S(2)}) copy-start(s32[256]{0:T(256)} %param.11) | copy-start | bytes 3076
  32.5 240.6 %all-to-all-start = ((bf16[720,4,1568]{2,0,1:T(8,128)(2,1)}), bf16[720,4,1568]{2,0,1:T(8,128)(2,1)}, u32[]{:S(2)}, u32[]{:S(2)}) async-start(bf16[720,4,1568]{2,0,1:T(8,128)(2,1)} %copy.11), calls=%async_computation | async-start | bytes 19169280 | tf_op jit(solution)/shard_map/all_to_all | solution.py:47
  39.0 93.6 %all-gather.10.cloned.1.call-start = ((), (), s32[]{:S(2)}) async-start(), calls=%async_computation.1 | async-start | bytes 1884160 | tf_op jit(solution)/shard_map/all_gather | solution.py:51
  273.1 8.3 %copy-start.3 = (s32[256]{0:T(256)S(1)}, s32[256]{0:T(256)}, u32[]{:S(2)}) copy-start(s32[256]{0:T(256)} %param.10) | copy-start | bytes 3076
  544.8 11.5 %copy-start.2 = (f32[64]{0:T(128)}, f32[64]{0:T(128)S(1)}, u32[]{:S(2)}) copy-start(f32[64]{0:T(128)S(1)} %get-tuple-element.257) | copy-start | bytes 772
  544.8 11.5 %copy-start.4 = (f32[64]{0:T(128)}, f32[64]{0:T(128)S(1)}, u32[]{:S(2)}) copy-start(f32[64]{0:T(128)S(1)} %get-tuple-element.256) | copy-start | bytes 772
Sparse Core Ops, SparseCore 0:
  41.3 91.1 all-gather.9
where the time goes:
time: 564 us; the launch traced here: 563 us
  blocking collectives  269 us (48%)
  waiting for transfers between devices  233 us (41%)
  local copies, waits for them, and re-layouts  26.3 us (5%)
  between operations  14.1 us (2%)
  matrix products  8.37 us (1%)
  starting transfers between devices  6.48 us (1%)
    all_gather x4, blocking collectives, merged(): gathered = jax.tree.map(lambda a: lax.all_gather(a, axis), part)  259 us
    all_to_all x1, waiting for transfers between devices, local(): lax.all_to_all(unembed, 'width', split_axis=1, concat_axis=0, tiled=True)  141 us
    all_gather x1, waiting for transfers between devices, local(): lax.all_gather(normed, 'width', axis=0, tiled=True)  92.2 us
    all_to_all x2, local copies, waits for them, and re-layouts, local(): lax.all_to_all(unembed, 'width', split_axis=1, concat_axis=0, tiled=True)  25.3 us
  transfers between devices with their start and end apart: 2, of which 2 were waited for; matrix products, arithmetic and copies ran while one was open for 0% of the time, Pallas kernels for 0%

commit v1 on v0

--- a/solution.py
+++ b/solution.py
@@ -44,14 +44,11 @@
     values = hidden.astype(jnp.float32)
     square = jnp.mean(values * values, axis=1, keepdims=True)
     normed = (values * lax.rsqrt(square + 1e-05) * gain[None, :]).astype(jnp.bfloat16)
-    columns = lax.all_to_all(unembed, "width", split_axis=1, concat_axis=0, tiled=True)
-    col_share = columns.shape[1]
+    own_features = lax.all_to_all(normed, "width", split_axis=1, concat_axis=0, tiled=True)
+    partial = jnp.dot(own_features, unembed, preferred_element_type=jnp.float32)
+    logits = lax.psum_scatter(partial, "width", scatter_dimension=1, tiled=True)
+    col_share = logits.shape[1]
     first_col = (lax.axis_index("vocab") * widths + owner) * col_share
-    logits = jnp.dot(
-        lax.all_gather(normed, "width", axis=0, tiled=True),
-        columns,
-        preferred_element_type=jnp.float32,
-    )
     stats = local_stats(logits, targets, first_col)
     all_max, all_total, all_weighted, all_target = merged(stats, ("vocab", "width"), combine_parts)
     row_start = owner * own_rows

time: 564 us -> 436 us (0.77)
  waiting for transfers between devices: 233 us -> 111 us
  local copies, waits for them, and re-layouts: 26.3 us -> 2.17 us
  blocking collectives: 269 us -> 289 us
  starting transfers between devices: 6.48 us -> 0.04 us
    all_to_all x1 -> x0, waiting for transfers between devices: 141 us -> none  [local(): lax.all_to_all(unembed, 'width', split_axis=1, concat_axis=0, tiled=True)]
    reduce_scatter x0 -> x1, waiting for transfers between devices: none -> 111 us  [local(): logits = lax.psum_scatter(partial, 'width', scatter_dimension=1, tiled=True)]
    all_gather x1 -> x0, waiting for transfers between devices: 92.2 us -> none  [local(): lax.all_gather(normed, 'width', axis=0, tiled=True)]
    all_to_all x2, local copies, waits for them, and re-layouts: 25.3 us -> 0.6 us  [local(): lax.all_to_all(normed, 'width', split_axis=1, concat_axis=0, tiled=True)]
    all_to_all x0 -> x1, blocking collectives: none -> 17.8 us  [local(): lax.all_to_all(normed, 'width', split_axis=1, concat_axis=0, tiled=True)]
    all_to_all x1 -> x0, starting transfers between devices: 6.48 us -> none  [local(): lax.all_to_all(unembed, 'width', split_axis=1, concat_axis=0, tiled=True)]
  transfers between devices with their start and end apart: 2 -> 1, of which waited for: 2 -> 1; matrix products, arithmetic and copies ran while one was open for 0% -> 0% of each run, Pallas kernels for 0% -> 0%
where the time goes in v1:
time: 436 us
  blocking collectives  289 us (66%)
  waiting for transfers between devices  111 us (25%)
  between operations  14.1 us (3%)
  matrix products  10.2 us (2%)
  other arithmetic  7.72 us (2%)
    all_gather x4, blocking collectives, merged(): gathered = jax.tree.map(lambda a: lax.all_gather(a, axis), part)  260 us
    reduce_scatter x1, waiting for transfers between devices, local(): logits = lax.psum_scatter(partial, 'width', scatter_dimension=1, tiled=True)  111 us
    all_to_all x1, blocking collectives, local(): lax.all_to_all(normed, 'width', split_axis=1, concat_axis=0, tiled=True)  17.8 us
    psum x1, blocking collectives, local(): lax.psum((jnp.dot(token_logprob, member, precision=lax.Precision.HIGHEST)...  10.6 us
    dot_general x1, matrix products, local(): partial = jnp.dot(own_features, unembed, preferred_element_type=jnp.float32)  10.1 us
  transfers between devices with their start and end apart: 1, of which 1 were waited for; matrix products, arithmetic and copies ran while one was open for 0% of the time, Pallas kernels for 0%

profile of v1, /device:TPU:0, one launch (start us, length us, event | category | flops | bytes accessed | tf_op | source)
XLA Modules:
  0.0 436.0 jit_solution(4553548483958127575)
XLA Ops:
  7.2 0.0 reduce-scatter.2.cloned.1.call-start
  7.2 1.2 fusion.1
  8.4 1.2 fusion.3
  9.6 0.6 all_to_all.14
  10.2 17.8 %all_to_all.19 = bf16[64,4,720]{2,0,1:T(8,128)(2,1)S(1)} all-to-all(bf16[64,4,720]{2,0,1:T(8,128)(2,1)S(1)} %copy.11), channel_id=1, replica_groups=mesh['vocab'=8,'width'=4] {'width'}, dimensions={1} | all-to-all | bytes 737280 | tf_op jit(solution)/shard_map/all_to_all | solution.py:47
  28.0 10.1 %fusion.6 = f32[256,6272]{0,1:T(8,128)} fusion(bf16[256,720]{1,0:T(8,128)(2,1)S(1)} %bitcast.42, bf16[720,6272]{1,0:T(8,128)(2,1)} %param.9), kind=kOutput, calls=%fused_computation.31 | convolution fusion | flops 2312110080 | bytes 15822848 | tf_op jit(solution)/shard_map/dot_general | solution.py:48
  38.1 0.0 reduce-scatter.2.cloned.1.call-update
  38.1 0.0 copy-start.2
  38.2 0.6 copy-done.4
  38.8 0.1 dynamic_slice.76
  38.9 0.1 convert_reduce_fusion
  39.0 111.3 %reduce-scatter.2.cloned.1.call-done = f32[256,1568]{0,1:T(8,128)} async-done(((f32[256,6272]{0,1:T(8,128)}), f32[256,1568]{0,1:T(8,128)}) %reduce-scatter.2.cloned.1.call-update) | async-done | bytes 1605648 | tf_op jit(solution)/shard_map/reduce_scatter | solution.py:49
  150.3 1.8 reduce_max.9
  152.1 67.5 %all-gather.4 = f32[32,1,256]{2,1,0:T(1,128)S(1)} all-gather(f32[1,1,256]{2,1,0:T(1,128)S(1)} %bitcast.56), channel_id=2, replica_groups=mesh['vocab'=8,'width'=4] {'vocab','width'}, dimensions={0}, use_global_device_ids=true | all-gather | bytes 33792 | tf_op jit(solution)/shard_map/all_gather | solution.py:10
  219.6 0.9 multiply_reduce_fusion
  220.5 63.6 %all-gather.5 = f32[32,1,256]{2,1,0:T(1,128)S(1)} all-gather(f32[1,1,256]{2,1,0:T(1,128)S(1)} %bitcast.59), channel_id=3, replica_groups=mesh['vocab'=8,'width'=4] {'vocab','width'}, dimensions={0}, use_global_device_ids=true | all-gather | bytes 33792 | tf_op jit(solution)/shard_map/all_gather | solution.py:10
  284.1 65.8 %all-gather.6 = f32[32,1,256]{2,1,0:T(1,128)S(1)} all-gather(f32[1,1,256]{2,1,0:T(1,128)S(1)} %bitcast.58), channel_id=4, replica_groups=mesh['vocab'=8,'width'=4] {'vocab','width'}, dimensions={0}, use_global_device_ids=true | all-gather | bytes 33792 | tf_op jit(solution)/shard_map/all_gather | solution.py:10
  349.9 63.5 %all-gather.7 = f32[32,1,256]{2,1,0:T(1,128)S(1)} all-gather(f32[1,1,256]{2,1,0:T(1,128)S(1)} %bitcast.57), channel_id=5, replica_groups=mesh['vocab'=8,'width'=4] {'vocab','width'}, dimensions={0}, use_global_device_ids=true | all-gather | bytes 33792 | tf_op jit(solution)/shard_map/all_gather | solution.py:10
  413.5 3.7 while.21
  417.2 0.1 dynamic-slice_subtract_fusion
  417.3 0.1 convolution_bitcast_fusion
  417.4 0.6 divide_subtract_fusion
  418.0 10.6 %all-reduce = (f32[48]{0:T(128)S(1)}, f32[48]{0:T(128)S(1)}) all-reduce(f32[48]{0:T(128)S(1)} %convolution_bitcast_fusion, f32[48]{0:T(128)S(1)} %convert_reduce_fusion), channel_id=1, replica_groups=mesh['vocab'=8,'width'=4] {'width'}, use_global_device_ids=true, to_apply=%region_8.9 | all-reduce | flops 96 | bytes 768 | tf_op jit(solution)/shard_map/psum | solution.py:64
  428.6 0.5 div.15
  (205 shorter events, 2.3 us)
Async XLA Ops:
  7.2 143.1 %reduce-scatter.2.cloned.1.call-start = ((), (), s32[]{:S(2)}) async-start(), calls=%async_computation.2 | async-start | bytes 8028160 | tf_op jit(solution)/shard_map/reduce_scatter | solution.py:49
  38.1 0.7 copy-start.4
  38.1 181.5 %copy-start.2 = (s32[256]{0:T(256)S(1)}, s32[256]{0:T(256)}, u32[]{:S(2)}) copy-start(s32[256]{0:T(256)} %param.10) | copy-start | bytes 3076
  150.3 69.3 %copy-start = (f32[256,1568]{0,1:T(8,128)S(1)}, f32[256,1568]{0,1:T(8,128)}, u32[]{:S(2)}) copy-start(f32[256,1568]{0,1:T(8,128)} %reduce-scatter.2.cloned.1.call-done) | copy-start | bytes 4816900
  417.3 11.9 %copy-start.1 = (f32[64]{0:T(128)}, f32[64]{0:T(128)S(1)}, u32[]{:S(2)}) copy-start(f32[64]{0:T(128)S(1)} %get-tuple-element.257) | copy-start | bytes 772
  417.3 11.9 %copy-start.3 = (f32[64]{0:T(128)}, f32[64]{0:T(128)S(1)}, u32[]{:S(2)}) copy-start(f32[64]{0:T(128)S(1)} %get-tuple-element.256) | copy-start | bytes 772
Sparse Core Ops, SparseCore 0:
  38.3 111.9 reduce-scatter.1

commit v2 on v1

v2 whole, which is shorter than its diff:
```python
import functools

import jax
import jax.numpy as jnp
from jax import lax
from jax.experimental import pallas as pl
from jax.experimental.pallas import tpu as pltpu
from jax.sharding import PartitionSpec as P

SEQS = 48
LANES = 128
LAG = 3
LOWEST = -1e38
MESH = pl.DeviceIdType.MESH


def kernel(
    n, nv, hidden_ref, gain_ref, unembed_ref, targets_ref, seq_ref, out_ref,
    weights, blocks, rows_in, buf, target_cols, state, packed, gathered, final,
    w_sem, own_sem, x_send, x_recv, c_send, c_recv, v_send, v_recv, f_send, f_recv,
):
    me = lax.axis_index("width")
    my_vocab = lax.axis_index("vocab")
    own_rows, width_dim = hidden_ref.shape
    share = width_dim // n
    half = (n // 2) * own_rows
    chunks = unembed_ref.shape[1] // LANES
    last = n - 1

    load_weights = pltpu.make_async_copy(unembed_ref, weights, w_sem)
    load_weights.start()

    barrier = pltpu.get_barrier_semaphore()
    for k in range(1, n):
        pl.semaphore_signal(
            barrier, inc=1, device_id={"width": lax.rem(me + k, n)}, device_id_type=MESH
        )
    for k in range(1, nv):
        pl.semaphore_signal(
            barrier, inc=1, device_id={"vocab": lax.rem(my_vocab + k, nv)}, device_id_type=MESH
        )

    values = hidden_ref[...].astype(jnp.float32)
    square = jnp.mean(values * values, axis=1, keepdims=True)
    normed = (values * lax.rsqrt(square + 1e-05) * gain_ref[...]).astype(jnp.bfloat16)
    for j in range(n):
        blocks[j] = normed[:, j * share : (j + 1) * share]

    pl.semaphore_wait(barrier, n - 1 + nv - 1)

    def row_copy(peer, source):
        return pltpu.make_async_remote_copy(
            src_ref=blocks.at[peer],
            dst_ref=rows_in.at[source],
            send_sem=x_send.at[peer],
            recv_sem=x_recv.at[source],
            device_id={"width": peer},
            device_id_type=MESH,
        )

    for k in range(1, n):
        row_copy(lax.rem(me + k, n), me).start()
    own = pltpu.make_async_copy(blocks.at[me], rows_in.at[me], own_sem)
    own.start()

    target_row = targets_ref[...].astype(jnp.float32)
    target_all = jnp.transpose(jnp.broadcast_to(target_row, (LANES, 2 * half)))
    target_cols[0] = target_all[:half]
    target_cols[1] = target_all[half:]
    state[0] = jnp.full((half, LANES), LOWEST, jnp.float32)
    for k in range(1, 4):
        state[k] = jnp.zeros((half, LANES), jnp.float32)

    own.wait()
    load_weights.wait()
    for k in range(1, n):
        peer = lax.rem(me + k, n)
        row_copy(peer, peer).wait_recv()

    def chunk_copy(side, c, peer):
        return pltpu.make_async_remote_copy(
            src_ref=buf.at[side, c],
            dst_ref=buf.at[side, c],
            send_sem=c_send.at[side, c],
            recv_sem=c_recv.at[side, c],
            device_id={"width": peer},
            device_id_type=MESH,
        )

    first_col = my_vocab * (chunks * LANES)
    lane = lax.broadcasted_iota(jnp.int32, (half, LANES), 1)

    def partial_logits(side, c):
        cols = pl.ds(pl.multiple_of(c * LANES, LANES), LANES)
        x = rows_in[side * (n // 2) : (side + 1) * (n // 2)].reshape(half, share)
        return jnp.dot(x, weights[:, cols], preferred_element_type=jnp.float32)

    def take_stats(side, c, logits):
        column = (first_col + c * LANES + lane).astype(jnp.float32)
        old_max = state[0]
        new_max = jnp.maximum(old_max, logits)
        scale = jnp.exp(old_max - new_max)
        shifted = jnp.exp(logits - new_max)
        state[0] = new_max
        state[1] = state[1] * scale + shifted
        state[2] = state[2] * scale + shifted * logits
        state[3] = state[3] + jnp.where(column == target_cols[side], logits, 0.0)

    def advance(side, c, head, tail, peer):
        @pl.when((c >= 0) & (c < chunks))
        def _():
            mine = partial_logits(side, c)

            @pl.when(me == head)
            def _():
                buf[side, c] = mine
                chunk_copy(side, c, peer).start()

            @pl.when(me != head)
            def _():
                chunk_copy(side, c, peer).wait_recv()
                total = buf[side, c] + mine

                @pl.when(me != tail)
                def _():
                    buf[side, c] = total
                    chunk_copy(side, c, peer).start()

                @pl.when(me == tail)
                def _():
                    take_stats(side, c, total)

    down = lax.rem(me + n - 1, n)
    up = lax.rem(me + 1, n)

    def step(s, carry):
        advance(0, s - (last - me) * LAG, last, 0, down)
        advance(1, s - me * LAG, 0, last, up)
        return carry

    lax.fori_loop(0, chunks + last * LAG, step, 0)

    def stats_copy(peer, source):
        return pltpu.make_async_remote_copy(
            src_ref=packed.at[0],
            dst_ref=gathered.at[source],
            send_sem=v_send.at[peer],
            recv_sem=v_recv.at[source],
            device_id={"vocab": peer},
            device_id_type=MESH,
        )

    def final_copy(side, peer):
        return pltpu.make_async_remote_copy(
            src_ref=packed.at[1],
            dst_ref=final.at[side],
            send_sem=f_send.at[peer],
            recv_sem=f_recv.at[side],
            device_id={"width": peer},
            device_id_type=MESH,
        )

    def finish(side):
        lane_max = state[0]
        row_max = jnp.max(lane_max, axis=1, keepdims=True)
        scale = jnp.exp(lane_max - row_max)
        columns = (
            row_max,
            jnp.sum(state[1] * scale, axis=1, keepdims=True),
            jnp.sum(state[2] * scale, axis=1, keepdims=True),
            jnp.sum(state[3], axis=1, keepdims=True),
        )
        wide = jnp.zeros((half, LANES), jnp.float32)
        for k in range(4):
            wide = jnp.where(lane == k, columns[k], wide)
        flat = jnp.transpose(wide)[:8]
        packed[0] = flat
        for k in range(1, nv):
            stats_copy(lax.rem(my_vocab + k, nv), my_vocab).start()
        gathered[my_vocab] = flat
        for k in range(1, nv):
            peer = lax.rem(my_vocab + k, nv)
            stats_copy(peer, peer).wait_recv()
        parts = [gathered[v] for v in range(nv)]
        top = functools.reduce(jnp.maximum, [part[0:1] for part in parts])
        total = jnp.zeros_like(top)
        weighted = jnp.zeros_like(top)
        target = jnp.zeros_like(top)
        for part in parts:
            factor = jnp.exp(part[0:1] - top)
            total = total + part[1:2] * factor
            weighted = weighted + part[2:3] * factor
            target = target + part[3:4]
        log_normalizer = top + jnp.log(total)
        rows = lax.broadcasted_iota(jnp.int32, (8, half), 0)
        result = jnp.where(
            rows == 0,
            log_normalizer,
            jnp.where(rows == 1, log_normalizer - weighted / total, target - log_normalizer),
        )
        packed[1] = result
        for k in range(1, n):
            final_copy(side, lax.rem(me + k, n)).start()
        final[side] = result

    @pl.when(me == 0)
    def _():
        finish(0)

    @pl.when(me == last)
    def _():
        finish(1)

    @pl.when(me != 0)
    def _():
        final_copy(0, 0).wait_recv()

    @pl.when(me != last)
    def _():
        final_copy(1, 0).wait_recv()

    ids = lax.broadcasted_iota(jnp.int32, (LANES, half), 0)
    sums = jnp.zeros((LANES, 1), jnp.float32)
    counts = jnp.zeros((LANES, 1), jnp.float32)
    for side in range(2):
        member = ids == seq_ref[:, side * half : (side + 1) * half]
        sums = sums + jnp.sum(jnp.where(member, final[side, 2:3], 0.0), axis=1, keepdims=True)
        counts = counts + jnp.sum(member.astype(jnp.float32), axis=1, keepdims=True)
    means = sums / jnp.maximum(counts, 1.0)
    out_ref[...] = jnp.zeros_like(out_ref)
    out_ref[3:4, :] = jnp.transpose(jnp.broadcast_to(means, (LANES, LANES)))[0:1]
    for w in range(n):

        @pl.when(me == w)
        def _():
            start = (w % (n // 2)) * own_rows
            out_ref[0:3, 0:own_rows] = final[w // (n // 2), 0:3, start : start + own_rows]

    for k in range(1, n):
        row_copy(lax.rem(me + k, n), me).wait_send()

    def drain(c, carry):
        @pl.when(me != 0)
        def _():
            chunk_copy(0, c, down).wait_send()

        @pl.when(me != last)
        def _():
            chunk_copy(1, c, up).wait_send()

        return carry

    lax.fori_loop(0, chunks, drain, 0)

    @pl.when((me == 0) | (me == last))
    def _():
        for k in range(1, nv):
            stats_copy(lax.rem(my_vocab + k, nv), my_vocab).wait_send()
        for k in range(1, n):
            final_copy(0, lax.rem(me + k, n)).wait_send()


def solution(mesh):
    n, nv = mesh.shape["width"], mesh.shape["vocab"]

    def local(hidden, gain, unembed, targets, seq_ids):
        own_rows, width_dim = hidden.shape
        share, columns = unembed.shape
        half = (n // 2) * own_rows
        chunks = columns // LANES
        vmem = pl.BlockSpec(memory_space=pltpu.VMEM)
        out = pl.pallas_call(
            functools.partial(kernel, n, nv),
            out_shape=jax.ShapeDtypeStruct((8, LANES), jnp.float32),
            in_specs=[vmem, vmem, pl.BlockSpec(memory_space=pl.ANY), vmem, vmem],
            out_specs=vmem,
            scratch_shapes=[
                pltpu.VMEM((share, columns), jnp.bfloat16),
                pltpu.VMEM((n, own_rows, share), jnp.bfloat16),
                pltpu.VMEM((n, own_rows, share), jnp.bfloat16),
                pltpu.VMEM((2, chunks, half, LANES), jnp.float32),
                pltpu.VMEM((2, half, LANES), jnp.float32),
                pltpu.VMEM((4, half, LANES), jnp.float32),
                pltpu.VMEM((2, 8, half), jnp.float32),
                pltpu.VMEM((nv, 8, half), jnp.float32),
                pltpu.VMEM((2, 8, half), jnp.float32),
                pltpu.SemaphoreType.DMA,
                pltpu.SemaphoreType.DMA,
                pltpu.SemaphoreType.DMA((n,)),
                pltpu.SemaphoreType.DMA((n,)),
                pltpu.SemaphoreType.DMA((2, chunks)),
                pltpu.SemaphoreType.DMA((2, chunks)),
                pltpu.SemaphoreType.DMA((nv,)),
                pltpu.SemaphoreType.DMA((nv,)),
                pltpu.SemaphoreType.DMA((n,)),
                pltpu.SemaphoreType.DMA((2,)),
            ],
            compiler_params=pltpu.CompilerParams(
                collective_id=0, has_side_effects=True, vmem_limit_bytes=66_000_000
            ),
        )(hidden, gain[None, :], unembed, targets[None, :], seq_ids[None, :])
        return out[0, :own_rows], out[1, :own_rows], out[2, :own_rows], out[3, :SEQS]

    return jax.shard_map(
        local,
        mesh=mesh,
        in_specs=(P("width", None), P(), P("width", "vocab"), P(), P()),
        out_specs=(P("width"), P("width"), P("width"), P()),
        check_vma=False,
    )
```

time: 436 us -> 110 us (0.25)
  blocking collectives: 289 us -> 0 us
  waiting for transfers between devices: 111 us -> 0 us
  Pallas kernels: 0 us -> 105 us
  between operations: 14.1 us -> 0.64 us
  matrix products: 10.2 us -> 0 us
  other arithmetic: 7.72 us -> 0 us
    all_gather x4 -> x0, blocking collectives: 260 us -> none  [merged(): gathered = jax.tree.map(lambda a: lax.all_gather(a, axis), part)]
    reduce_scatter x1 -> x0, waiting for transfers between devices: 111 us -> none  [local(): logits = lax.psum_scatter(partial, 'width', scatter_dimension=1, tiled=True)]
    pallas_call x0 -> x1, Pallas kernels: none -> 105 us  [local(): pl.pallas_call(functools.partial(kernel, n, nv), out_shape=jax.ShapeDtype...]
    all_to_all x1 -> x0, blocking collectives: 17.8 us -> none  [local(): lax.all_to_all(normed, 'width', split_axis=1, concat_axis=0, tiled=True)]
    psum x1 -> x0, blocking collectives: 10.6 us -> none  [local(): lax.psum((jnp.dot(token_logprob, member, precision=lax.Precision.HIGHEST)...]
    dot_general x2 -> x0, matrix products: 10.2 us -> none  [the longest x1 10.1 us: local(): partial = jnp.dot(own_features, unembed, preferred_element_type=jnp.float32)]
  transfers between devices with their start and end apart: 1 -> 0, of which waited for: 1 -> 0; matrix products, arithmetic and copies ran while one was open for 0% -> 0% of each run, Pallas kernels for 0% -> 0%
where the time goes in v2:
time: 110 us; the launch traced here: 109 us
  Pallas kernels  105 us (95%)
  local copies, waits for them, and re-layouts  3.8 us (3%)
    pallas_call x1, Pallas kernels, local(): pl.pallas_call(functools.partial(kernel, n, nv), out_shape=jax.ShapeDtype...  105 us

profile of v2, /device:TPU:0, one launch (start us, length us, event | category | flops | bytes accessed | tf_op | source)
XLA Modules:
  0.0 109.4 jit_solution(3587517199913935061)
XLA Ops:
  0.6 1.3 %broadcast_in_dim.9.gain_ref = f32[1,2880]{1,0:T(1,128)} reshape(f32[2880]{0:T(1024)} %param.6) | data formatting | bytes 23040 | tf_op jit(solution)/shard_map/broadcast_in_dim | solution.py:301
  1.9 105.0 %shard_map.84 = f32[8,128]{1,0:T(8,128)} custom-call(bf16[64,2880]{1,0:T(8,128)(2,1)} %hidden_ref.1, f32[1,2880]{1,0:T(1,128)} %broadcast_in_dim.9.gain_ref, bf16[720,6272]{1,0:T(8,128)(2,1)} %unembed_ref.1, s32[1,256]{1,0:T(1,128)} %bitcast.10, s32[1,256]{1,0:T(1,128)} %bitcast.11), custom_call_target="tpu_custom_call" | custom-call | tf_op jit(solution)/shard_map/pallas_call | solution.py:272
  106.9 1.2 %slice_bitcast_fusion = f32[48]{0:T(128)} fusion(f32[8,128]{1,0:T(8,128)} %shard_map.84), kind=kLoop, calls=%fused_computation | loop fusion | bytes 384 | tf_op jit(solution)/shard_map/squeeze | solution.py:302
  108.1 1.3 %slice_bitcast_fusion.1 = (f32[64]{0:T(128)}, f32[64]{0:T(128)}, f32[64]{0:T(128)}) fusion(f32[8,128]{1,0:T(8,128)} %shard_map.84), kind=kLoop, calls=%fused_computation.1 | loop fusion | bytes 1536 | tf_op jit(solution)/shard_map/squeeze | solution.py:302

commit v3 on v2

--- a/solution.py
+++ b/solution.py
@@ -9,9 +9,15 @@
 
 SEQS = 48
 LANES = 128
-LAG = 3
+LAG = 5
+GROUPS = 2
 LOWEST = -1e38
 MESH = pl.DeviceIdType.MESH
+
+
+def send_order(me, n):
+    sign = jnp.where(me < n // 2, -1, 1)
+    return [lax.rem(me + sign * k + n, n) for k in range(1, n)]
 
 
 def kernel(
@@ -26,9 +32,18 @@
     half = (n // 2) * own_rows
     chunks = unembed_ref.shape[1] // LANES
     last = n - 1
-
-    load_weights = pltpu.make_async_copy(unembed_ref, weights, w_sem)
-    load_weights.start()
+    group_blocks = n // 2 // GROUPS
+    group_rows = group_blocks * own_rows
+    items = GROUPS * chunks
+    slots = last * LAG + 1
+
+    early = chunks // 7 * LANES
+    loads = []
+    for k, cols in enumerate((pl.ds(0, early), pl.ds(early, chunks * LANES - early))):
+        loads.append(
+            pltpu.make_async_copy(unembed_ref.at[:, cols], weights.at[:, cols], w_sem.at[k])
+        )
+        loads[k].start()
 
     barrier = pltpu.get_barrier_semaphore()
     for k in range(1, n):
@@ -42,7 +57,7 @@
 
     values = hidden_ref[...].astype(jnp.float32)
     square = jnp.mean(values * values, axis=1, keepdims=True)
-    normed = (values * lax.rsqrt(square + 1e-05) * gain_ref[...]).astype(jnp.bfloat16)
+    normed = (values * lax.rsqrt(square + 1e-05) * gain_ref[...][None, :]).astype(jnp.bfloat16)
     for j in range(n):
         blocks[j] = normed[:, j * share : (j + 1) * share]
 
@@ -58,8 +73,8 @@
             device_id_type=MESH,
         )
 
-    for k in range(1, n):
-        row_copy(lax.rem(me + k, n), me).start()
+    for peer in send_order(me, n):
+        row_copy(peer, me).start()
     own = pltpu.make_async_copy(blocks.at[me], rows_in.at[me], own_sem)
     own.start()
 
@@ -72,73 +87,94 @@
         state[k] = jnp.zeros((half, LANES), jnp.float32)
 
     own.wait()
-    load_weights.wait()
-    for k in range(1, n):
-        peer = lax.rem(me + k, n)
-        row_copy(peer, peer).wait_recv()
+    loads[0].wait()
 
     def chunk_copy(side, c, peer):
         return pltpu.make_async_remote_copy(
             src_ref=buf.at[side, c],
             dst_ref=buf.at[side, c],
-            send_sem=c_send.at[side, c],
-            recv_sem=c_recv.at[side, c],
+            send_sem=c_send.at[side, lax.rem(c, slots)],
+            recv_sem=c_recv.at[side, lax.rem(c, slots)],
             device_id={"width": peer},
             device_id_type=MESH,
         )
 
     first_col = my_vocab * (chunks * LANES)
     lane = lax.broadcasted_iota(jnp.int32, (half, LANES), 1)
-
-    def partial_logits(side, c):
+    item_lane = lax.broadcasted_iota(jnp.int32, (group_rows, LANES), 1)
+
+    def partial_logits(first_block, c):
         cols = pl.ds(pl.multiple_of(c * LANES, LANES), LANES)
-        x = rows_in[side * (n // 2) : (side + 1) * (n // 2)].reshape(half, share)
+        x = rows_in[pl.ds(first_block, group_blocks)].reshape(group_rows, share)
         return jnp.dot(x, weights[:, cols], preferred_element_type=jnp.float32)
 
-    def take_stats(side, c, logits):
-        column = (first_col + c * LANES + lane).astype(jnp.float32)
-        old_max = state[0]
+    def take_stats(side, first_block, c, logits):
+        rows = pl.ds(pl.multiple_of((first_block - side * (n // 2)) * own_rows, 8), group_rows)
+        column = (first_col + c * LANES + item_lane).astype(jnp.float32)
+        old_max = state[0, rows]
         new_max = jnp.maximum(old_max, logits)
         scale = jnp.exp(old_max - new_max)
         shifted = jnp.exp(logits - new_max)
-        state[0] = new_max
-        state[1] = state[1] * scale + shifted
-        state[2] = state[2] * scale + shifted * logits
-        state[3] = state[3] + jnp.where(column == target_cols[side], logits, 0.0)
-
-    def advance(side, c, head, tail, peer):
-        @pl.when((c >= 0) & (c < chunks))
-        def _():
-            mine = partial_logits(side, c)
+        state[0, rows] = new_max
+        state[1, rows] = state[1, rows] * scale + shifted
+        state[2, rows] = state[2, rows] * scale + shifted * logits
+        state[3, rows] = state[3, rows] + jnp.where(column == target_cols[side, rows], logits, 0.0)
+
+    def advance(side, item, head, tail, peer):
+        @pl.when((item >= 0) & (item < items))
+        def _():
+            group = item // chunks
+            c = item - group * chunks
+            first_block = group * group_blocks if side == 0 else n - (group + 1) * group_blocks
+            for g in range(GROUPS):
+                start = g * group_blocks if side == 0 else n - (g + 1) * group_blocks
+
+                @pl.when(item == g * chunks)
+                def _():
+                    for w in range(start, start + group_blocks):
+
+                        @pl.when(me != w)
+                        def _():
+                            row_copy(w, w).wait_recv()
+
+            mine = partial_logits(first_block, c)
+
+            @pl.when((me != tail) & (item >= slots))
+            def _():
+                chunk_copy(side, item - slots, peer).wait_send()
 
             @pl.when(me == head)
             def _():
-                buf[side, c] = mine
-                chunk_copy(side, c, peer).start()
+                buf[side, item] = mine
+                chunk_copy(side, item, peer).start()
 
             @pl.when(me != head)
             def _():
-                chunk_copy(side, c, peer).wait_recv()
-                total = buf[side, c] + mine
+                chunk_copy(side, item, peer).wait_recv()
+                total = buf[side, item] + mine
 
                 @pl.when(me != tail)
                 def _():
-                    buf[side, c] = total
-                    chunk_copy(side, c, peer).start()
+                    buf[side, item] = total
+                    chunk_copy(side, item, peer).start()
 
                 @pl.when(me == tail)
                 def _():
-                    take_stats(side, c, total)
+                    take_stats(side, first_block, c, total)
 
     down = lax.rem(me + n - 1, n)
     up = lax.rem(me + 1, n)
 
     def step(s, carry):
-        advance(0, s - (last - me) * LAG, last, 0, down)
-        advance(1, s - me * LAG, 0, last, up)
+        @pl.when(s == 1)
+        def _():
+            loads[1].wait()
+
+        advance(0, s - me * LAG, 0, last, up)
+        advance(1, s - (last - me) * LAG, last, 0, down)
         return carry
 
-    lax.fori_loop(0, chunks + last * LAG, step, 0)
+    lax.fori_loop(0, items + last * LAG, step, 0)
 
     def stats_copy(peer, source):
         return pltpu.make_async_remote_copy(
@@ -203,19 +239,19 @@
             final_copy(side, lax.rem(me + k, n)).start()
         final[side] = result
 
+    @pl.when(me == last)
+    def _():
+        finish(0)
+
     @pl.when(me == 0)
     def _():
-        finish(0)
-
-    @pl.when(me == last)
-    def _():
         finish(1)
 
+    @pl.when(me != last)
+    def _():
+        final_copy(0, 0).wait_recv()
+
     @pl.when(me != 0)
-    def _():
-        final_copy(0, 0).wait_recv()
-
-    @pl.when(me != last)
     def _():
         final_copy(1, 0).wait_recv()
 
@@ -240,17 +276,17 @@
         row_copy(lax.rem(me + k, n), me).wait_send()
 
     def drain(c, carry):
+        @pl.when(me != last)
+        def _():
+            chunk_copy(0, c, up).wait_send()
+
         @pl.when(me != 0)
         def _():
-            chunk_copy(0, c, down).wait_send()
-
-        @pl.when(me != last)
-        def _():
-            chunk_copy(1, c, up).wait_send()
+            chunk_copy(1, c, down).wait_send()
 
         return carry
 
-    lax.fori_loop(0, chunks, drain, 0)
+    lax.fori_loop(max(items - slots, 0), items, drain, 0)
 
     @pl.when((me == 0) | (me == last))
     def _():
@@ -267,7 +303,7 @@
         own_rows, width_dim = hidden.shape
         share, columns = unembed.shape
         half = (n // 2) * own_rows
-        chunks = columns // LANES
+        items = GROUPS * (columns // LANES)
         vmem = pl.BlockSpec(memory_space=pltpu.VMEM)
         out = pl.pallas_call(
             functools.partial(kernel, n, nv),
@@ -278,18 +314,18 @@
                 pltpu.VMEM((share, columns), jnp.bfloat16),
                 pltpu.VMEM((n, own_rows, share), jnp.bfloat16),
                 pltpu.VMEM((n, own_rows, share), jnp.bfloat16),
-                pltpu.VMEM((2, chunks, half, LANES), jnp.float32),
+                pltpu.VMEM((2, items, half // GROUPS, LANES), jnp.float32),
                 pltpu.VMEM((2, half, LANES), jnp.float32),
                 pltpu.VMEM((4, half, LANES), jnp.float32),
                 pltpu.VMEM((2, 8, half), jnp.float32),
                 pltpu.VMEM((nv, 8, half), jnp.float32),
                 pltpu.VMEM((2, 8, half), jnp.float32),
-                pltpu.SemaphoreType.DMA,
+                pltpu.SemaphoreType.DMA((2,)),
                 pltpu.SemaphoreType.DMA,
                 pltpu.SemaphoreType.DMA((n,)),
                 pltpu.SemaphoreType.DMA((n,)),
-                pltpu.SemaphoreType.DMA((2, chunks)),
-                pltpu.SemaphoreType.DMA((2, chunks)),
+                pltpu.SemaphoreType.DMA((2, (n - 1) * LAG + 1)),
+                pltpu.SemaphoreType.DMA((2, (n - 1) * LAG + 1)),
                 pltpu.SemaphoreType.DMA((nv,)),
                 pltpu.SemaphoreType.DMA((nv,)),
                 pltpu.SemaphoreType.DMA((n,)),
@@ -298,7 +334,7 @@
             compiler_params=pltpu.CompilerParams(
                 collective_id=0, has_side_effects=True, vmem_limit_bytes=66_000_000
             ),
-        )(hidden, gain[None, :], unembed, targets[None, :], seq_ids[None, :])
+        )(hidden, gain, unembed, targets[None, :], seq_ids[None, :])
         return out[0, :own_rows], out[1, :own_rows], out[2, :own_rows], out[3, :SEQS]
 
     return jax.shard_map(

time: 110 us -> 102 us (0.927)
  Pallas kernels: 105 us -> 98.4 us
  local copies, waits for them, and re-layouts: 3.8 us -> 2.49 us
    pallas_call x1, Pallas kernels: 105 us -> 98.4 us  [local(): pl.pallas_call(functools.partial(kernel, n, nv), out_shape=jax.ShapeDtype...]
    broadcast_in_dim x1 -> x0, local copies, waits for them, and re-layouts: 1.32 us -> none  [local(): gain[None, :]]
where the time goes in v3:
time: 102 us
  Pallas kernels  98.4 us (96%)
  local copies, waits for them, and re-layouts  2.49 us (2%)
    pallas_call x1, Pallas kernels, local(): pl.pallas_call(functools.partial(kernel, n, nv), out_shape=jax.ShapeDtype...  98.4 us

profile of v3, /device:TPU:0, one launch (start us, length us, event | category | flops | bytes accessed | tf_op | source)
XLA Modules:
  0.0 101.5 jit_solution(156902131090974134)
XLA Ops:
  0.6 98.4 %shard_map.84 = f32[8,128]{1,0:T(8,128)} custom-call(bf16[64,2880]{1,0:T(8,128)(2,1)} %hidden_ref.1, f32[2880]{0:T(1024)} %gain_ref.1, bf16[720,6272]{1,0:T(8,128)(2,1)} %unembed_ref.1, s32[1,256]{1,0:T(1,128)} %bitcast.10, s32[1,256]{1,0:T(1,128)} %bitcast.11), custom_call_target="tpu_custom_call" | custom-call | tf_op jit(solution)/shard_map/pallas_call | solution.py:308
  99.0 1.3 %slice_bitcast_fusion.1 = (f32[64]{0:T(128)}, f32[64]{0:T(128)}, f32[64]{0:T(128)}) fusion(f32[8,128]{1,0:T(8,128)} %shard_map.84), kind=kLoop, calls=%fused_computation.1 | loop fusion | bytes 1536 | tf_op jit(solution)/shard_map/squeeze | solution.py:338
  100.3 1.2 %slice_bitcast_fusion = f32[48]{0:T(128)} fusion(f32[8,128]{1,0:T(8,128)} %shard_map.84), kind=kLoop, calls=%fused_computation | loop fusion | bytes 384 | tf_op jit(solution)/shard_map/squeeze | solution.py:338

commit v4 on v3

--- a/solution.py
+++ b/solution.py
@@ -15,15 +15,10 @@
 MESH = pl.DeviceIdType.MESH
 
 
-def send_order(me, n):
-    sign = jnp.where(me < n // 2, -1, 1)
-    return [lax.rem(me + sign * k + n, n) for k in range(1, n)]
-
-
 def kernel(
     n, nv, hidden_ref, gain_ref, unembed_ref, targets_ref, seq_ref, out_ref,
     weights, blocks, rows_in, buf, target_cols, state, packed, gathered, final,
-    w_sem, own_sem, x_send, x_recv, c_send, c_recv, v_send, v_recv, f_send, f_recv,
+    w_sem, own_sem, x_send, x_recv, p_send, p_recv, c_send, c_recv, v_send, v_recv, f_send, f_recv,
 ):
     me = lax.axis_index("width")
     my_vocab = lax.axis_index("vocab")
@@ -63,18 +58,42 @@
 
     pl.semaphore_wait(barrier, n - 1 + nv - 1)
 
+    my_part = pl.ds(pl.multiple_of(lax.rem(my_vocab, 2) * (own_rows // 2), own_rows // 2), own_rows // 2)
+    other_part = pl.ds(
+        pl.multiple_of((1 - lax.rem(my_vocab, 2)) * (own_rows // 2), own_rows // 2), own_rows // 2
+    )
+    partner = my_vocab + 1 - 2 * lax.rem(my_vocab, 2)
+
     def row_copy(peer, source):
         return pltpu.make_async_remote_copy(
-            src_ref=blocks.at[peer],
-            dst_ref=rows_in.at[source],
+            src_ref=blocks.at[peer, my_part],
+            dst_ref=rows_in.at[source, my_part],
             send_sem=x_send.at[peer],
             recv_sem=x_recv.at[source],
             device_id={"width": peer},
             device_id_type=MESH,
         )
 
-    for peer in send_order(me, n):
-        row_copy(peer, me).start()
+    def pass_rows(source, part):
+        return pltpu.make_async_remote_copy(
+            src_ref=rows_in.at[source, part],
+            dst_ref=rows_in.at[source, part],
+            send_sem=p_send.at[source],
+            recv_sem=p_recv.at[source],
+            device_id={"vocab": partner},
+            device_id_type=MESH,
+        )
+
+    def send_rows():
+        for k in range(1, n):
+            row_copy(lax.rem(me + jnp.where(me < n // 2, k, n - k), n), me).start()
+
+    rows_now = jnp.where(me < n // 2, me, last - me) < group_blocks
+
+    @pl.when(rows_now)
+    def _():
+        send_rows()
+
     own = pltpu.make_async_copy(blocks.at[me], rows_in.at[me], own_sem)
     own.start()
 
@@ -129,13 +148,22 @@
             for g in range(GROUPS):
                 start = g * group_blocks if side == 0 else n - (g + 1) * group_blocks
 
+                @pl.when(item == g * (chunks // 2))
+                def _():
+                    for w in range(start, start + group_blocks):
+
+                        @pl.when(me != w)
+                        def _():
+                            row_copy(w, w).wait_recv()
+                            pass_rows(w, my_part).start()
+
                 @pl.when(item == g * chunks)
                 def _():
                     for w in range(start, start + group_blocks):
 
                         @pl.when(me != w)
                         def _():
-                            row_copy(w, w).wait_recv()
+                            pass_rows(w, other_part).wait_recv()
 
             mine = partial_logits(first_block, c)
 
@@ -169,6 +197,10 @@
         @pl.when(s == 1)
         def _():
             loads[1].wait()
+
+        @pl.when((s == 2 * LAG) & jnp.logical_not(rows_now))
+        def _():
+            send_rows()
 
         advance(0, s - me * LAG, 0, last, up)
         advance(1, s - (last - me) * LAG, last, 0, down)
@@ -274,6 +306,7 @@
 
     for k in range(1, n):
         row_copy(lax.rem(me + k, n), me).wait_send()
+        pass_rows(lax.rem(me + k, n), my_part).wait_send()
 
     def drain(c, carry):
         @pl.when(me != last)
@@ -324,6 +357,8 @@
                 pltpu.SemaphoreType.DMA,
                 pltpu.SemaphoreType.DMA((n,)),
                 pltpu.SemaphoreType.DMA((n,)),
+                pltpu.SemaphoreType.DMA((n,)),
+                pltpu.SemaphoreType.DMA((n,)),
                 pltpu.SemaphoreType.DMA((2, (n - 1) * LAG + 1)),
                 pltpu.SemaphoreType.DMA((2, (n - 1) * LAG + 1)),
                 pltpu.SemaphoreType.DMA((nv,)),

time: 102 us -> 101 us (level)
  Pallas kernels: 98.4 us -> 97.2 us
    pallas_call x1, Pallas kernels: 98.4 us -> 97.2 us  [local(): pl.pallas_call(functools.partial(kernel, n, nv), out_shape=jax.ShapeDtype...]
where the time goes in v4:
time: 101 us; the launch traced here: 100 us
  Pallas kernels  97.2 us (96%)
  local copies, waits for them, and re-layouts  2.49 us (2%)
    pallas_call x1, Pallas kernels, local(): pl.pallas_call(functools.partial(kernel, n, nv), out_shape=jax.ShapeDtype...  97.2 us

profile of v4, /device:TPU:0, one launch (start us, length us, event | category | flops | bytes accessed | tf_op | source)
XLA Modules:
  0.0 100.3 jit_solution(10837190758252981300)
XLA Ops:
  0.6 97.2 %shard_map.84 = f32[8,128]{1,0:T(8,128)} custom-call(bf16[64,2880]{1,0:T(8,128)(2,1)} %hidden_ref.1, f32[2880]{0:T(1024)} %gain_ref.1, bf16[720,6272]{1,0:T(8,128)(2,1)} %unembed_ref.1, s32[1,256]{1,0:T(1,128)} %bitcast.10, s32[1,256]{1,0:T(1,128)} %bitcast.11), custom_call_target="tpu_custom_call" | custom-call | tf_op jit(solution)/shard_map/pallas_call | solution.py:341
  97.9 1.3 %slice_bitcast_fusion.1 = (f32[64]{0:T(128)}, f32[64]{0:T(128)}, f32[64]{0:T(128)}) fusion(f32[8,128]{1,0:T(8,128)} %shard_map.84), kind=kLoop, calls=%fused_computation.1 | loop fusion | bytes 1536 | tf_op jit(solution)/shard_map/squeeze | solution.py:373
  99.2 1.2 %slice_bitcast_fusion = f32[48]{0:T(128)} fusion(f32[8,128]{1,0:T(8,128)} %shard_map.84), kind=kLoop, calls=%fused_computation | loop fusion | bytes 384 | tf_op jit(solution)/shard_map/squeeze | solution.py:373
